TPU v7x, 32 devices: a whole 2x2x4 slice. The times are simulated.
32 devices in a mesh: band: 4 (over z), ga: 8 (over y, x, core).
Axes of the slice: x: 2, y: 2, z: 4, core: 2. Of those that a mesh axis runs over, the one named last changes fastest.
Arguments:
- coeffs: float32 [2, 4, 18432], P(None, 'band', 'ga'), may hold values from -8 to 8
- cell_map: int32 [18432], P('ga'), may hold values from 0 to 110591, as said below
- potential: float32 [96, 96, 96], P(None, 'ga'), may hold values from -2 to 1
- projectors: float32 [2, 64, 18432], P(None, None, 'ga'), may hold values from -6 to 6
- strengths: float32 [8, 8, 8], replicated, may hold values from -2 to 2
- proj_atom: int32 [64], replicated, may hold values from 0 to 7, as said below
- proj_chan: int32 [64], replicated, may hold values from 0 to 7, as said below
Outputs:
- new_bands: float32 [2, 4, 18432], P(None, 'band', 'ga')
- energy: float32 [4], P('band')
- residual_norm: float32 [4], P('band')
- correlation: float32 [2, 4, 4], P(None, 'band')
- subspace: float32 [2, 4, 4], P(None, 'band')
Inputs may be any that keep to these rules, and one draw needn't show every extreme that they name: `cell_map`: in block d (entries d * 2304 to (d + 1) * 2304 - 1) the entries are distinct cells (i * 96 + y) * 96 + z of grid planes x = d + 8 * i. `proj_atom`: each pair of atom and channel belongs to exactly one projector. `proj_chan`: each pair of atom and channel belongs to exactly one projector.
All inputs are finite; a program needn't handle non-finite values.
Results may differ from a plain program's by a relative error of at most 0.0002.
Values sent between devices are 32-bit elements; how exact they have to be, the bound alone decides.
No kernel may reach another device: no remote copies, remote signals or barrier semaphores. Data moves between devices by JAX's collectives and lax.ppermute only.
A program may use at most 64 MiB of HBM per device.

v0:
```python
import jax
import jax.numpy as jnp
from jax import lax
from jax.sharding import PartitionSpec as P

top_precision = lax.Precision.HIGHEST
kin_unit = 0.02
small_eps = 1e-06


def signed_freq(index_arr, grid_len):
    return jnp.where(index_arr < grid_len // 2, index_arr, index_arr - grid_len)


def wave_tables(grid_len, row_freq, col_freq, sign_val, factor):
    phase = row_freq[:, None] * col_freq[None, :] % grid_len
    angle = 2.0 * jnp.pi / grid_len * phase.astype(jnp.float32)
    return (jnp.cos(angle) * factor, jnp.sin(angle) * (sign_val * factor))


def block_table(cos_table, sin_table):
    upper = jnp.concatenate([cos_table, sin_table], axis=1)
    lower = jnp.concatenate([-sin_table, cos_table], axis=1)
    return jnp.concatenate([upper, lower], axis=0)


def quarter_turn(grid_vals):
    half_len = grid_vals.shape[-1] // 2
    return jnp.concatenate([-grid_vals[..., half_len:], grid_vals[..., :half_len]], axis=-1)


def mix_dim(grid_vals, cos_table, sin_table, pattern):
    direct = jnp.einsum(pattern, cos_table, grid_vals, precision=top_precision)
    turned = jnp.einsum(pattern, sin_table, quarter_turn(grid_vals), precision=top_precision)
    return direct + turned


def mix_last(grid_vals, table_full):
    row_width = grid_vals.shape[-1]
    product = jnp.dot(
        grid_vals.reshape(-1, row_width),
        table_full,
        precision=top_precision,
        preferred_element_type=jnp.float32,
    )
    return product.reshape(grid_vals.shape)


def band_dot(left_vec, right_vec, weight):
    return jnp.sum(left_vec * right_vec * weight, axis=(0, 2))


def per_band(values):
    return values[None, :, None]


def pair_products(left_vec, right_vec):

    def contract(first_part, second_part):
        return jnp.einsum("bg,cg->bc", first_part, second_part, precision=top_precision)

    real_part = contract(left_vec[0], right_vec[0]) + contract(left_vec[1], right_vec[1])
    imag_part = contract(left_vec[0], right_vec[1]) - contract(left_vec[1], right_vec[0])
    return jnp.stack([real_part, imag_part])


def precondition(residual, kinetic, kin_level):
    x_ratio = kinetic[None, :] / (1.5 * kin_level[:, None] + 1.0)
    numer_poly = 27.0 + x_ratio * (18.0 + x_ratio * (12.0 + 8.0 * x_ratio))
    square = x_ratio * x_ratio
    return residual * (numer_poly / (numer_poly + 16.0 * square * square))[None]


def coupling_matrix(proj_atom, proj_chan, strengths):
    atom_count = strengths.shape[0]
    chan_count = strengths.shape[1]
    symmetric = 0.5 * (strengths + jnp.swapaxes(strengths, 1, 2))
    atom_hot = (proj_atom[:, None] == jnp.arange(atom_count, dtype=jnp.int32)[None, :]).astype(
        jnp.float32
    )
    chan_hot = (proj_chan[:, None] == jnp.arange(chan_count, dtype=jnp.int32)[None, :]).astype(
        jnp.float32
    )
    rows_d = jnp.einsum("pa,pc,acd->pd", atom_hot, chan_hot, symmetric, precision=top_precision)
    same_atom = jnp.dot(
        atom_hot, atom_hot.T, precision=top_precision, preferred_element_type=jnp.float32
    )
    return same_atom * jnp.dot(
        rows_d, chan_hot.T, precision=top_precision, preferred_element_type=jnp.float32
    )


def combine(term_list):
    merged = {}
    for scalar, coef_map in term_list:
        for index_one, coef_a in coef_map.items():
            merged[index_one] = merged.get(index_one, 0.0) + scalar * coef_a
    return merged


def gram_form(gram_table, left_map, right_map, use_kin):
    running = 0.0
    for index_one, coef_a in left_map.items():
        for index_two, coef_b in right_map.items():
            running = running + coef_a * coef_b * gram_table[use_kin, index_one, index_two]
    return running


def new_pairs(first_new, last_new, kinds):
    pair_list = []
    for use_kin in kinds:
        for index_two in range(first_new, last_new):
            for index_one in range(index_two + 1):
                pair_list.append((index_one, index_two, use_kin))
    return pair_list


def body(coeffs, cell_map, potential, projectors, strengths, proj_atom, proj_chan):
    ga_count = lax.axis_size("ga")
    grid_len = potential.shape[0]
    planes = grid_len // ga_count
    band_local = coeffs.shape[1]
    total_pw = coeffs.shape[2] * ga_count
    device = lax.axis_index("ga")
    plane_num = cell_map // (grid_len * grid_len)
    y_index = cell_map // grid_len % grid_len
    z_index = cell_map % grid_len
    freq_x = signed_freq(device + ga_count * plane_num, grid_len)
    freq_y = signed_freq(y_index, grid_len)
    freq_z = signed_freq(z_index, grid_len)
    kinetic = kin_unit * (freq_x * freq_x + freq_y * freq_y + freq_z * freq_z).astype(jnp.float32)
    kin_weight = kinetic[None, None, :]
    slot_re = (plane_num * grid_len + y_index) * (2 * grid_len) + z_index
    slot_im = slot_re + grid_len
    cell_count = planes * grid_len * 2 * grid_len
    natural = jnp.arange(grid_len, dtype=jnp.int32)
    cyclic = natural % planes * ga_count + natural // planes
    cos_fwd, sin_fwd = wave_tables(grid_len, natural, natural, 1.0, 1.0)
    cos_back, sin_back = wave_tables(grid_len, natural, natural, -1.0, 1.0 / grid_len)
    z_forward = block_table(cos_fwd, sin_fwd)
    z_backward = block_table(cos_back, sin_back)
    xcos_fwd, xsin_fwd = wave_tables(grid_len, natural, cyclic, 1.0, 1.0)
    xcos_back, xsin_back = wave_tables(grid_len, cyclic, natural, -1.0, 1.0 / grid_len)
    doubled = jnp.concatenate([potential, potential], axis=-1)
    coupling = coupling_matrix(proj_atom, proj_chan, strengths)

    def real_space(grid_vals):
        grid_vals = mix_dim(grid_vals, xcos_fwd, xsin_fwd, "kj,bjyw->bkyw")
        grid_vals = grid_vals * doubled[None]
        grid_vals = mix_dim(grid_vals, xcos_back, xsin_back, "jk,bkyw->bjyw")
        return lax.all_to_all(grid_vals, "ga", split_axis=1, concat_axis=2, tiled=True)

    def local_part(vectors):
        item_count = vectors.shape[1]
        flat_grid = jnp.zeros((item_count, cell_count), jnp.float32)
        flat_grid = flat_grid.at[:, slot_re].set(vectors[0]).at[:, slot_im].set(vectors[1])
        grid_vals = mix_last(
            flat_grid.reshape(item_count, planes, grid_len, 2 * grid_len), z_forward
        )
        grid_vals = mix_dim(grid_vals, cos_fwd, sin_fwd, "ky,bpyw->bpkw")
        grid_vals = real_space(
            lax.all_to_all(grid_vals, "ga", split_axis=2, concat_axis=1, tiled=True)
        )
        grid_vals = mix_dim(grid_vals, cos_back, sin_back, "ky,bpyw->bpkw")
        flat_grid = mix_last(grid_vals, z_backward).reshape(item_count, cell_count)
        return jnp.stack([flat_grid[:, slot_re], flat_grid[:, slot_im]])

    def contract(first_part, second_part):
        return jnp.einsum("pg,bg->pb", first_part, second_part, precision=top_precision)

    def spread(weights, proj_table):
        return jnp.einsum("pb,pg->bg", weights, proj_table, precision=top_precision)

    def projected_part(vectors):
        proj_re = contract(projectors[0], vectors[0]) + contract(projectors[1], vectors[1])
        proj_im = contract(projectors[0], vectors[1]) - contract(projectors[1], vectors[0])
        proj_re, proj_im = lax.psum((proj_re, proj_im), "ga")
        mixed_re = jnp.dot(
            coupling,
            proj_re / total_pw,
            precision=top_precision,
            preferred_element_type=jnp.float32,
        )
        mixed_im = jnp.dot(
            coupling,
            proj_im / total_pw,
            precision=top_precision,
            preferred_element_type=jnp.float32,
        )
        out_re = spread(mixed_re, projectors[0]) - spread(mixed_im, projectors[1])
        out_im = spread(mixed_re, projectors[1]) + spread(mixed_im, projectors[0])
        return jnp.stack([out_re, out_im])

    def apply_h(vectors):
        return kin_weight * vectors + local_part(vectors) + projected_part(vectors)

    def gram_sums(basis, pair_list):
        stacked = []
        for index_one, index_two, use_kin in pair_list:
            stacked.append(
                band_dot(basis[index_one], basis[index_two], kin_weight if use_kin else 1.0)
            )
        summed = lax.psum(jnp.stack(stacked), "ga") / total_pw
        found = {}
        for slot_num, entry in enumerate(pair_list):
            index_one, index_two, use_kin = entry
            found[use_kin, index_one, index_two] = summed[slot_num]
            found[use_kin, index_two, index_one] = summed[slot_num]
        return found

    def realize(coef_map, basis):
        running = jnp.zeros_like(basis[0])
        for index_one, coef_a in coef_map.items():
            running = (
                running
                + per_band(jnp.zeros((band_local,), jnp.float32) + coef_a) * basis[index_one]
            )
        return running

    h_zero = apply_h(coeffs)
    basis = [coeffs, h_zero]
    gram_table = gram_sums(basis, new_pairs(0, 2, (False, True)))
    psi_map = {0: 1.0}
    ham_map = {1: 1.0}
    eps_zero = gram_form(gram_table, psi_map, ham_map, False) / (
        gram_form(gram_table, psi_map, psi_map, False) + small_eps
    )
    r_map = combine([(1.0, ham_map), (-eps_zero, psi_map)])
    level_zero = gram_form(gram_table, r_map, r_map, True) / (
        gram_form(gram_table, r_map, r_map, False) + small_eps
    )
    p_zero = precondition(realize(r_map, basis), kinetic, level_zero)
    g_zero = apply_h(p_zero)
    basis = [coeffs, h_zero, p_zero, g_zero]
    gram_table.update(gram_sums(basis, new_pairs(2, 4, (False, True))))
    q_map = combine([(1.0, {3: 1.0}), (-eps_zero, {2: 1.0})])
    lam_zero = -gram_form(gram_table, r_map, q_map, False) / (
        gram_form(gram_table, q_map, q_map, False) + small_eps
    )
    psi_one_map = combine([(1.0, psi_map), (lam_zero, {2: 1.0})])
    h_one_map = combine([(1.0, ham_map), (lam_zero, {3: 1.0})])
    eps_one = gram_form(gram_table, psi_one_map, h_one_map, False) / (
        gram_form(gram_table, psi_one_map, psi_one_map, False) + small_eps
    )
    r_one_map = combine([(1.0, h_one_map), (-eps_one, psi_one_map)])
    change_map = combine([(1.0, r_map), (-1.0, r_one_map)])
    weight_one = gram_form(gram_table, r_map, change_map, False) / (
        gram_form(gram_table, change_map, change_map, False) + small_eps
    )
    step_mid = weight_one * lam_zero
    psi_mid_map = combine([(1.0, psi_map), (step_mid, {2: 1.0})])
    h_mid_map = combine([(1.0, ham_map), (step_mid, {3: 1.0})])
    r_mid_map = combine([(1.0, r_map), (-weight_one, change_map)])
    eps_mid = gram_form(gram_table, psi_mid_map, h_mid_map, False) / (
        gram_form(gram_table, psi_mid_map, psi_mid_map, False) + small_eps
    )
    level_mid = gram_form(gram_table, r_mid_map, r_mid_map, True) / (
        gram_form(gram_table, r_mid_map, r_mid_map, False) + small_eps
    )
    p_one = precondition(realize(r_mid_map, basis), kinetic, level_mid)
    g_one = apply_h(p_one)
    basis = [coeffs, h_zero, p_zero, g_zero, p_one, g_one]
    gram_table.update(gram_sums(basis, new_pairs(4, 6, (False,))))
    q_one_map = combine([(1.0, {5: 1.0}), (-eps_mid, {4: 1.0})])
    lam_one = -gram_form(gram_table, r_mid_map, q_one_map, False) / (
        gram_form(gram_table, q_one_map, q_one_map, False) + small_eps
    )
    new_map = combine([(1.0, psi_mid_map), (lam_one, {4: 1.0})])
    ham_new_map = combine([(1.0, h_mid_map), (lam_one, {5: 1.0})])
    norm_new = gram_form(gram_table, new_map, new_map, False) + small_eps
    energy = gram_form(gram_table, new_map, ham_new_map, False) / norm_new
    resid_map = combine([(1.0, ham_new_map), (-energy, new_map)])
    residual_norm = gram_form(gram_table, resid_map, resid_map, False) / norm_new
    new_bands = realize(new_map, basis)
    new_ham = realize(ham_new_map, basis)
    blank_rows = jnp.zeros((2, band_local, band_local * lax.axis_size("band")), jnp.float32)
    first_row = jnp.int32(0)
    over_rows = blank_rows
    ham_rows = blank_rows
    piece_bands = lax.all_gather(new_bands, "band", axis=1, tiled=True)
    piece_ham = lax.all_gather(new_ham, "band", axis=1, tiled=True)
    over_rows = lax.dynamic_update_slice_in_dim(
        over_rows, pair_products(new_bands, piece_bands), first_row, 2
    )
    ham_rows = lax.dynamic_update_slice_in_dim(
        ham_rows, pair_products(new_bands, piece_ham), first_row, 2
    )
    over_rows, ham_rows = (over_rows, ham_rows)
    over_rows, ham_rows = lax.psum((over_rows, ham_rows), "ga")
    correlation = over_rows / total_pw
    subspace = ham_rows / total_pw
    return (new_bands, energy, residual_norm, correlation, subspace)


def solution(mesh):
    placed = (
        P(None, "band", "ga"),
        P("ga"),
        P(None, "ga", None),
        P(None, None, "ga"),
        P(),
        P(),
        P(),
    )
    return jax.shard_map(
        body,
        mesh=mesh,
        in_specs=placed,
        out_specs=(
            P(None, "band", "ga"),
            P("band"),
            P("band"),
            P(None, "band", None),
            P(None, "band", None),
        ),
        check_vma=False,
    )
```

profile of v0, /device:TPU:0, one launch (start us, length us, event | category | flops | bytes accessed | tf_op | source)
XLA Modules:
  0.0 576.9 jit_solution(5087216117158828302)
XLA Ops:
  2.7 9.2 %scatter_custom_fusion = f32[221184]{0:T(1024)S(1)} fusion(s32[2304]{0:T(1024)S(1)} %compare_select_fusion.1, f32[2304]{0:T(1024)S(1)} %get-tuple-element.59, f32[]{:T(128)} %constant.112.clone.1), kind=kCustom, calls=%fused_computation.173 | custom fusion | bytes 884740 | tf_op jit(solution)/shard_map/scatter | solution.py:156
  11.9 9.4 %scatter_fusion = f32[221184]{0:T(1024)S(1)} fusion(f32[221184]{0:T(1024)S(1)} %scatter_custom_fusion, s32[2304]{0:T(1024)S(1)} %get-tuple-element.71, f32[2304]{0:T(1024)S(1)} %get-tuple-element.58), kind=kCustom, calls=%fused_computation.7 | custom fusion | bytes 36864 | tf_op jit(solution)/shard_map/scatter | solution.py:156
  22.7 2.4 fusion.159
  25.4 2.7 fusion.8
  30.3 5.3 all-to-all-start
  38.7 20.2 %all-reduce.3 = (f32[64,1]{0,1:T(1,128)S(1)}, f32[64,1]{0,1:T(1,128)S(1)}) all-reduce(f32[64,1]{0,1:T(1,128)S(1)} %fusion.53, f32[64,1]{0,1:T(1,128)S(1)} %fusion.51), channel_id=1, replica_groups=mesh['band'=4,'ga'=8] {'ga'}, use_global_device_ids=true, to_apply=%region_3.4 | all-reduce | flops 128 | bytes 1024 | tf_op jit(solution)/shard_map/psum | solution.py:177
  68.4 3.6 fusion.436
  76.2 2.4 fusion.150
  82.8 2.5 copy.153
  85.3 3.7 all-to-all-start.1
  90.7 15.1 %all-to-all-done.1 = f32[1,96,12,192]{3,0,2,1:T(1,128)S(1)} async-done(((f32[1,96,12,192]{3,0,2,1:T(1,128)}), f32[1,96,12,192]{3,0,2,1:T(1,128)S(1)}, u32[]{:S(2)}, u32[]{:S(2)}) %all-to-all-start.1) | async-done | bytes 884768 | tf_op jit(solution)/shard_map/all_to_all | solution.py:151
  108.2 2.4 fusion.435
  111.9 2.7 fusion.135
  117.9 12.3 %gather_fusion = f32[2304]{0:T(1024)S(1)} fusion(f32[221184]{0:T(1024)S(1)} %reshape.529, s32[3072]{0:T(1024)S(1)} %pad_clamp_fusion.1), kind=kCustom, calls=%fused_computation | custom fusion | bytes 27648 | tf_op jit(solution)/shard_map/gather | solution.py:166
  130.3 12.3 %gather_fusion.1 = f32[2304]{0:T(1024)S(1)} fusion(f32[221184]{0:T(1024)S(1)} %reshape.529, s32[3072]{0:T(1024)S(1)} %pad_clamp_fusion), kind=kCustom, calls=%fused_computation.1 | custom fusion | bytes 27648 | tf_op jit(solution)/shard_map/gather | solution.py:166
  143.5 4.0 stack.186
  147.5 11.8 %psum.79 = f32[6,1]{0,1:T(1,128)S(1)} all-reduce(f32[6,1]{0,1:T(1,128)S(1)} %stack.186), channel_id=1, replica_groups=mesh['band'=4,'ga'=8] {'ga'}, use_global_device_ids=true, to_apply=%region_10.11 | all-reduce | flops 6 | bytes 48 | tf_op jit(solution)/shard_map/psum | solution.py:203
  165.2 9.4 %scatter_custom_fusion.2 = f32[221184]{0:T(1024)S(1)} fusion(s32[2304]{0:T(1024)} %copy-done.57, f32[2304]{0:T(1024)S(1)} %get-tuple-element.56, f32[]{:T(128)} %constant.112.clone.1), kind=kCustom, calls=%fused_computation.171 | custom fusion | bytes 885248 | tf_op jit(solution)/shard_map/scatter | solution.py:156
  174.6 9.5 %scatter_fusion.1 = f32[221184]{0:T(1024)S(1)} fusion(f32[221184]{0:T(1024)S(1)} %scatter_custom_fusion.2, s32[2304]{0:T(1024)S(1)} %get-tuple-element.71, f32[2304]{0:T(1024)S(1)} %get-tuple-element.55), kind=kCustom, calls=%fused_computation.9 | custom fusion | bytes 36864 | tf_op jit(solution)/shard_map/scatter | solution.py:156
  186.2 2.4 fusion.157
  188.8 2.7 fusion.5
  193.7 3.6 all-to-all-start.2
  199.5 21.5 %all-reduce.2 = (f32[64,1]{0,1:T(1,128)}, f32[64,1]{0,1:T(1,128)}) all-reduce(f32[64,1]{0,1:T(1,128)S(1)} %fusion.49, f32[64,1]{0,1:T(1,128)S(1)} %fusion.47), channel_id=1, replica_groups=mesh['band'=4,'ga'=8] {'ga'}, use_global_device_ids=true, to_apply=%region_16.17 | all-reduce | flops 128 | bytes 1024 | tf_op jit(solution)/shard_map/psum | solution.py:177
  225.9 3.8 fusion.148
  229.7 2.4 fusion.434
  243.6 4.1 all-to-all-start.3
  251.6 12.8 %all-to-all-done.3 = f32[1,96,12,192]{3,0,2,1:T(1,128)S(1)} async-done(((f32[1,96,12,192]{3,0,2,1:T(1,128)}), f32[1,96,12,192]{3,0,2,1:T(1,128)S(1)}, u32[]{:S(2)}, u32[]{:S(2)}) %all-to-all-start.3) | async-done | bytes 884768 | tf_op jit(solution)/shard_map/all_to_all | solution.py:151
  275.0 12.3 %gather_fusion.2 = f32[2304]{0:T(1024)S(1)} fusion(f32[221184]{0:T(1024)S(1)} %reshape.549, s32[3072]{0:T(1024)S(1)} %copy-done.54), kind=kCustom, calls=%fused_computation.2 | custom fusion | bytes 27648 | tf_op jit(solution)/shard_map/gather | solution.py:166
  287.4 12.3 %gather_fusion.3 = f32[2304]{0:T(1024)S(1)} fusion(f32[221184]{0:T(1024)S(1)} %reshape.549, s32[3072]{0:T(1024)S(1)} %copy-done.51), kind=kCustom, calls=%fused_computation.3 | custom fusion | bytes 27648 | tf_op jit(solution)/shard_map/gather | solution.py:166
  300.7 8.8 %stack.207 = f32[14,1]{0,1:T(1,128)S(1)} concatenate(f32[1,1]{0,1:T(1,128)} %bitcast.65, f32[1,1]{0,1:T(1,128)} %bitcast.66, f32[1,1]{0,1:T(1,128)} %bitcast.67, f32[1,1]{0,1:T(1,128)} %bitcast.105, f32[1,1]{0,1:T(1,128)} %bitcast.106, f32[1,1]{0,1:T(1,128)} %bitcast.107, f32[1,1]{0,1:T(1,128)} %bitcast.108, f32[1,1]{0,1:T(1,128)} %bitcast.109, f32[1,1]{0,1:T(1,128)} %bitcast.110, ...), dimensions={0} | concatenate | bytes 112 | tf_op jit(solution)/shard_map/stack | solution.py:203
  310.0 11.8 %psum.82 = f32[14,1]{0,1:T(1,128)S(1)} all-reduce(f32[14,1]{0,1:T(1,128)S(1)} %stack.207), channel_id=1, replica_groups=mesh['band'=4,'ga'=8] {'ga'}, use_global_device_ids=true, to_apply=%region_29.30 | all-reduce | flops 14 | bytes 112 | tf_op jit(solution)/shard_map/psum | solution.py:203
  353.6 9.4 %scatter_custom_fusion.4 = f32[221184]{0:T(1024)S(1)} fusion(s32[2304]{0:T(1024)} %copy-done.57, f32[2304]{0:T(1024)S(1)} %get-tuple-element.54, f32[]{:T(128)} %constant.112.clone.1), kind=kCustom, calls=%fused_computation.169 | custom fusion | bytes 885248 | tf_op jit(solution)/shard_map/scatter | solution.py:156
  363.0 9.5 %scatter_fusion.2 = f32[221184]{0:T(1024)S(1)} fusion(f32[221184]{0:T(1024)S(1)} %scatter_custom_fusion.4, s32[2304]{0:T(1024)S(1)} %get-tuple-element.71, f32[2304]{0:T(1024)S(1)} %get-tuple-element.53), kind=kCustom, calls=%fused_computation.11 | custom fusion | bytes 36864 | tf_op jit(solution)/shard_map/scatter | solution.py:156
  374.6 2.4 fusion.155
  377.2 2.7 fusion.2
  382.1 3.6 all-to-all-start.4
  388.0 20.9 %all-reduce.1 = (f32[64,1]{0,1:T(1,128)S(1)}, f32[64,1]{0,1:T(1,128)S(1)}) all-reduce(f32[64,1]{0,1:T(1,128)S(1)} %fusion.45, f32[64,1]{0,1:T(1,128)S(1)} %fusion.43), channel_id=1, replica_groups=mesh['band'=4,'ga'=8] {'ga'}, use_global_device_ids=true, to_apply=%region_37.38 | all-reduce | flops 128 | bytes 1024 | tf_op jit(solution)/shard_map/psum | solution.py:177
  413.7 3.8 fusion.146
  417.5 2.4 fusion.432
  431.5 3.9 all-to-all-start.5
  443.2 9.0 %all-to-all-done.5 = f32[1,96,12,192]{3,0,2,1:T(1,128)S(1)} async-done(((f32[1,96,12,192]{3,0,2,1:T(1,128)}), f32[1,96,12,192]{3,0,2,1:T(1,128)S(1)}, u32[]{:S(2)}, u32[]{:S(2)}) %all-to-all-start.5) | async-done | bytes 884768 | tf_op jit(solution)/shard_map/all_to_all | solution.py:151
  462.7 12.3 %gather_fusion.4 = f32[2304]{0:T(1024)S(1)} fusion(f32[221184]{0:T(1024)S(1)} %reshape.569, s32[3072]{0:T(1024)S(1)} %copy-done.55), kind=kCustom, calls=%fused_computation.4 | custom fusion | bytes 27648 | tf_op jit(solution)/shard_map/gather | solution.py:166
  475.1 12.3 %gather_fusion.5 = f32[2304]{0:T(1024)S(1)} fusion(f32[221184]{0:T(1024)S(1)} %reshape.569, s32[3072]{0:T(1024)S(1)} %copy-done.52), kind=kCustom, calls=%fused_computation.5 | custom fusion | bytes 27648 | tf_op jit(solution)/shard_map/gather | solution.py:166
  488.3 7.0 %stack.225 = f32[11,1]{0,1:T(1,128)S(1)} concatenate(f32[1,1]{0,1:T(1,128)} %bitcast.136, f32[1,1]{0,1:T(1,128)} %bitcast.137, f32[1,1]{0,1:T(1,128)} %bitcast.138, f32[1,1]{0,1:T(1,128)} %bitcast.139, f32[1,1]{0,1:T(1,128)} %bitcast.140, f32[1,1]{0,1:T(1,128)} %bitcast.178, f32[1,1]{0,1:T(1,128)} %bitcast.179, f32[1,1]{0,1:T(1,128)} %bitcast.180, f32[1,1]{0,1:T(1,128)} %bitcast.181, ...), dimensions={0} | concatenate | bytes 88 | tf_op jit(solution)/shard_map/stack | solution.py:203
  495.9 11.8 %psum.85 = f32[11,1]{0,1:T(1,128)S(1)} all-reduce(f32[11,1]{0,1:T(1,128)S(1)} %stack.225), channel_id=1, replica_groups=mesh['band'=4,'ga'=8] {'ga'}, use_global_device_ids=true, to_apply=%region_45.46 | all-reduce | flops 11 | bytes 88 | tf_op jit(solution)/shard_map/psum | solution.py:203
  525.3 13.4 %all_gather.7 = f32[2,4,2304]{2,0,1:T(2,128)S(1)} all-gather(f32[2,1,2304]{2,0,1:T(2,128)S(1)} %multiply_add_fusion), channel_id=1, replica_groups=mesh['band'=4,'ga'=8] {'band'}, dimensions={1}, use_global_device_ids=true | all-gather | bytes 92160 | tf_op jit(solution)/shard_map/all_gather | solution.py:281
  538.8 13.2 %all_gather.6 = f32[2,4,2304]{2,0,1:T(2,128)S(1)} all-gather(f32[2,1,2304]{2,0,1:T(2,128)S(1)} %multiply_add_fusion.1), channel_id=1, replica_groups=mesh['band'=4,'ga'=8] {'band'}, dimensions={1}, use_global_device_ids=true | all-gather | bytes 92160 | tf_op jit(solution)/shard_map/all_gather | solution.py:280
  554.9 11.8 %all-reduce = (f32[2,1,4]{2,1,0:T(1,128)S(1)}, f32[2,1,4]{2,1,0:T(1,128)S(1)}) all-reduce(f32[2,1,4]{2,1,0:T(1,128)S(1)} %pad_maximum_fusion, f32[2,1,4]{2,1,0:T(1,128)S(1)} %pad_maximum_fusion.1), channel_id=1, replica_groups=mesh['band'=4,'ga'=8] {'ga'}, use_global_device_ids=true, to_apply=%region_46.47 | all-reduce | flops 16 | bytes 128 | tf_op jit(solution)/shard_map/psum | solution.py:289
  (312 shorter events, 116.0 us)
Async XLA Ops:
  0.9 20.7 %copy-start.31 = (f32[96,96]{1,0:T(8,128)}, f32[96,96]{1,0:T(8,128)S(1)}, u32[]{:S(2)}) copy-start(f32[96,96]{1,0:T(8,128)S(1)} %get-tuple-element.134) | copy-start | bytes 110596
  0.9 20.7 %copy-start.34 = (f32[96,96]{1,0:T(8,128)}, f32[96,96]{1,0:T(8,128)S(1)}, u32[]{:S(2)}) copy-start(f32[96,96]{1,0:T(8,128)S(1)} %get-tuple-element.135) | copy-start | bytes 110596
  1.1 20.5 %copy-start.37 = (f32[96,96]{1,0:T(8,128)}, f32[96,96]{1,0:T(8,128)S(1)}, u32[]{:S(2)}) copy-start(f32[96,96]{1,0:T(8,128)S(1)} %fusion.244) | copy-start | bytes 110596
  1.9 19.4 %copy-start.57 = (s32[2304]{0:T(1024)}, s32[2304]{0:T(1024)S(1)}, u32[]{:S(2)}) copy-start(s32[2304]{0:T(1024)S(1)} %compare_select_fusion.1) | copy-start | bytes 27652
  30.3 5.3 copy-start
  30.3 5.3 copy-start.16
  30.3 33.2 %all-to-all-start = ((f32[1,12,96,192]{3,0,1,2:T(1,128)}), f32[1,12,96,192]{3,0,1,2:T(1,128)S(1)}, u32[]{:S(2)}, u32[]{:S(2)}) async-start(f32[1,12,96,192]{3,0,1,2:T(1,128)} %copy.144), calls=%async_computation | async-start | bytes 2359296 | tf_op jit(solution)/shard_map/all_to_all | solution.py:162
  38.7 23.1 %copy-start.13 = (f32[64,64]{1,0:T(8,128)}, f32[64,64]{1,0:T(8,128)S(1)}, u32[]{:S(2)}) copy-start(f32[64,64]{1,0:T(8,128)S(1)} %convolution_multiply_fusion) | copy-start | bytes 49156
  60.3 18.3 %copy-start.1 = (f32[96,12,96]{0,2,1:T(8,128)}, f32[96,12,96]{0,2,1:T(8,128)S(1)}, u32[]{:S(2)}) copy-start(f32[96,12,96]{0,2,1:T(8,128)S(1)} %copy.151) | copy-start | bytes 1327108
  85.3 4.1 copy-start.59
  85.3 4.8 copy-start.58
  85.3 5.3 copy-start.45
  85.3 20.4 %all-to-all-start.1 = ((f32[1,96,12,192]{3,0,2,1:T(1,128)}), f32[1,96,12,192]{3,0,2,1:T(1,128)S(1)}, u32[]{:S(2)}, u32[]{:S(2)}) async-start(f32[1,96,12,192]{3,0,2,1:T(1,128)} %copy.153), calls=%async_computation.1 | async-start | bytes 2359296 | tf_op jit(solution)/shard_map/all_to_all | solution.py:151
  90.1 27.8 %copy-start.53 = (s32[3072]{0:T(1024)}, s32[3072]{0:T(1024)S(1)}, u32[]{:S(2)}) copy-start(s32[3072]{0:T(1024)S(1)} %pad_clamp_fusion.1) | copy-start | bytes 36868
  90.1 40.2 %copy-start.50 = (s32[3072]{0:T(1024)}, s32[3072]{0:T(1024)S(1)}, u32[]{:S(2)}) copy-start(s32[3072]{0:T(1024)S(1)} %pad_clamp_fusion) | copy-start | bytes 36868
  90.3 25.8 %copy-start.22 = (f32[96,96]{1,0:T(8,128)}, f32[96,96]{1,0:T(8,128)S(1)}, u32[]{:S(2)}) copy-start(f32[96,96]{1,0:T(8,128)S(1)} %fusion.245) | copy-start | bytes 110596
  90.6 25.5 %copy-start.25 = (f32[96,96]{1,0:T(8,128)}, f32[96,96]{1,0:T(8,128)S(1)}, u32[]{:S(2)}) copy-start(f32[96,96]{1,0:T(8,128)S(1)} %get-tuple-element.136) | copy-start | bytes 110596
  90.6 25.5 %copy-start.28 = (f32[96,96]{1,0:T(8,128)}, f32[96,96]{1,0:T(8,128)S(1)}, u32[]{:S(2)}) copy-start(f32[96,96]{1,0:T(8,128)S(1)} %get-tuple-element.137) | copy-start | bytes 110596
  90.7 52.0 %copy-start.47 = (f32[2304]{0:T(1024)}, f32[2304]{0:T(1024)S(1)}, u32[]{:S(2)}) copy-start(f32[2304]{0:T(1024)S(1)} %fusion.272) | copy-start | bytes 27652
  130.3 12.4 %copy-start.17 = (f32[2,1,2304]{2,1,0:T(1,128)S(1)}, f32[2,1,2304]{2,1,0:T(1,128)}, u32[]{:S(2)}) copy-start(f32[2,1,2304]{2,1,0:T(1,128)} %param.7) | copy-start | bytes 55300
  130.3 12.4 %copy-start.62 = (f32[1,1,2304]{2,0,1:T(1,128)S(1)}, f32[1,1,2304]{2,0,1:T(1,128)}, u32[]{:S(2)}) copy-start(f32[1,1,2304]{2,0,1:T(1,128)} %stack.178) | copy-start | bytes 27652
  130.3 12.4 %copy-start.63 = (f32[1,1,2304]{2,0,1:T(1,128)S(1)}, f32[1,1,2304]{2,0,1:T(1,128)}, u32[]{:S(2)}) copy-start(f32[1,1,2304]{2,0,1:T(1,128)} %stack.179) | copy-start | bytes 27652
  143.5 21.8 %copy-start.40 = (f32[2,1,2304]{2,0,1:T(2,128)}, f32[2,1,2304]{2,0,1:T(2,128)S(1)}, u32[]{:S(2)}) copy-start(f32[2,1,2304]{2,0,1:T(2,128)S(1)} %get-tuple-element.70) | copy-start | bytes 55300
  165.1 33.8 %copy-start.10 = (f32[2,1,2304]{2,0,1:T(2,128)}, f32[2,1,2304]{2,0,1:T(2,128)S(1)}, u32[]{:S(2)}) copy-start(f32[2,1,2304]{2,0,1:T(2,128)S(1)} %add_multiply_fusion.1) | copy-start | bytes 55300
  193.7 27.3 %all-to-all-start.2 = ((f32[1,12,96,192]{3,0,1,2:T(1,128)}), f32[1,12,96,192]{3,0,1,2:T(1,128)S(1)}, u32[]{:S(2)}, u32[]{:S(2)}) async-start(f32[1,12,96,192]{3,0,1,2:T(1,128)} %copy.166), calls=%async_computation.2 | async-start | bytes 2359296 | tf_op jit(solution)/shard_map/all_to_all | solution.py:162
  243.6 4.1 copy-start.14
  243.6 4.1 copy-start.69
  243.6 5.4 copy-start.68
  243.6 20.8 %all-to-all-start.3 = ((f32[1,96,12,192]{3,0,2,1:T(1,128)}), f32[1,96,12,192]{3,0,2,1:T(1,128)S(1)}, u32[]{:S(2)}, u32[]{:S(2)}) async-start(f32[1,96,12,192]{3,0,2,1:T(1,128)} %copy.173), calls=%async_computation.3 | async-start | bytes 2359296 | tf_op jit(solution)/shard_map/all_to_all | solution.py:151
  275.0 12.3 %copy-start.51 = (s32[3072]{0:T(1024)S(1)}, s32[3072]{0:T(1024)}, u32[]{:S(2)}) copy-start(s32[3072]{0:T(1024)} %copy-done.50) | copy-start | bytes 36868
  287.3 12.4 %copy-start.11 = (f32[2,1,2304]{2,0,1:T(2,128)S(1)}, f32[2,1,2304]{2,0,1:T(2,128)}, u32[]{:S(2)}) copy-start(f32[2,1,2304]{2,0,1:T(2,128)} %copy-done.10) | copy-start | bytes 55300
  287.4 12.4 %copy-start.18 = (f32[2,1,2304]{2,1,0:T(1,128)S(1)}, f32[2,1,2304]{2,1,0:T(1,128)}, u32[]{:S(2)}) copy-start(f32[2,1,2304]{2,1,0:T(1,128)} %param.7) | copy-start | bytes 55300
  287.4 12.4 %copy-start.41 = (f32[2,1,2304]{2,0,1:T(2,128)S(1)}, f32[2,1,2304]{2,0,1:T(2,128)}, u32[]{:S(2)}) copy-start(f32[2,1,2304]{2,0,1:T(2,128)} %copy-done.40) | copy-start | bytes 55300
  287.4 12.4 %copy-start.48 = (f32[2304]{0:T(1024)S(1)}, f32[2304]{0:T(1024)}, u32[]{:S(2)}) copy-start(f32[2304]{0:T(1024)} %copy-done.47) | copy-start | bytes 27652
  287.4 12.4 %copy-start.60 = (f32[1,1,2304]{2,0,1:T(1,128)S(1)}, f32[1,1,2304]{2,0,1:T(1,128)}, u32[]{:S(2)}) copy-start(f32[1,1,2304]{2,0,1:T(1,128)} %stack.193) | copy-start | bytes 27652
  287.4 12.4 %copy-start.61 = (f32[1,1,2304]{2,0,1:T(1,128)S(1)}, f32[1,1,2304]{2,0,1:T(1,128)}, u32[]{:S(2)}) copy-start(f32[1,1,2304]{2,0,1:T(1,128)} %stack.194) | copy-start | bytes 27652
  287.4 66.1 %copy-start.46 = (s32[2304]{0:T(1024)S(1)}, s32[2304]{0:T(1024)}, u32[]{:S(2)}) copy-start(s32[2304]{0:T(1024)} %param.8) | copy-start | bytes 27652
  300.7 62.3 %copy-start.43 = (f32[2,1,2304]{2,0,1:T(2,128)}, f32[2,1,2304]{2,0,1:T(2,128)S(1)}, u32[]{:S(2)}) copy-start(f32[2,1,2304]{2,0,1:T(2,128)S(1)} %get-tuple-element.69) | copy-start | bytes 55300
  353.6 33.8 %copy-start.20 = (f32[2,1,2304]{2,0,1:T(2,128)}, f32[2,1,2304]{2,0,1:T(2,128)S(1)}, u32[]{:S(2)}) copy-start(f32[2,1,2304]{2,0,1:T(2,128)S(1)} %add_multiply_fusion) | copy-start | bytes 55300
  382.1 26.8 %all-to-all-start.4 = ((f32[1,12,96,192]{3,0,1,2:T(1,128)}), f32[1,12,96,192]{3,0,1,2:T(1,128)S(1)}, u32[]{:S(2)}, u32[]{:S(2)}) async-start(f32[1,12,96,192]{3,0,1,2:T(1,128)} %copy.185), calls=%async_computation.4 | async-start | bytes 2359296 | tf_op jit(solution)/shard_map/all_to_all | solution.py:162
  431.5 20.7 %all-to-all-start.5 = ((f32[1,96,12,192]{3,0,2,1:T(1,128)}), f32[1,96,12,192]{3,0,2,1:T(1,128)S(1)}, u32[]{:S(2)}, u32[]{:S(2)}) async-start(f32[1,96,12,192]{3,0,2,1:T(1,128)} %copy.192), calls=%async_computation.5 | async-start | bytes 2359296 | tf_op jit(solution)/shard_map/all_to_all | solution.py:151
  462.7 12.3 %copy-start.52 = (s32[3072]{0:T(1024)S(1)}, s32[3072]{0:T(1024)}, u32[]{:S(2)}) copy-start(s32[3072]{0:T(1024)} %copy-done.50) | copy-start | bytes 36868
  475.0 12.4 %copy-start.12 = (f32[2,1,2304]{2,0,1:T(2,128)S(1)}, f32[2,1,2304]{2,0,1:T(2,128)}, u32[]{:S(2)}) copy-start(f32[2,1,2304]{2,0,1:T(2,128)} %copy-done.10) | copy-start | bytes 55300
  475.0 12.4 %copy-start.19 = (f32[2,1,2304]{2,1,0:T(1,128)S(1)}, f32[2,1,2304]{2,1,0:T(1,128)}, u32[]{:S(2)}) copy-start(f32[2,1,2304]{2,1,0:T(1,128)} %param.7) | copy-start | bytes 55300
  475.1 12.4 %copy-start.21 = (f32[2,1,2304]{2,0,1:T(2,128)S(1)}, f32[2,1,2304]{2,0,1:T(2,128)}, u32[]{:S(2)}) copy-start(f32[2,1,2304]{2,0,1:T(2,128)} %copy-done.20) | copy-start | bytes 55300
  475.1 12.4 %copy-start.42 = (f32[2,1,2304]{2,0,1:T(2,128)S(1)}, f32[2,1,2304]{2,0,1:T(2,128)}, u32[]{:S(2)}) copy-start(f32[2,1,2304]{2,0,1:T(2,128)} %copy-done.40) | copy-start | bytes 55300
  475.1 12.4 %copy-start.44 = (f32[2,1,2304]{2,0,1:T(2,128)S(1)}, f32[2,1,2304]{2,0,1:T(2,128)}, u32[]{:S(2)}) copy-start(f32[2,1,2304]{2,0,1:T(2,128)} %copy-done.43) | copy-start | bytes 55300
  475.1 12.4 %copy-start.49 = (f32[2304]{0:T(1024)S(1)}, f32[2304]{0:T(1024)}, u32[]{:S(2)}) copy-start(f32[2304]{0:T(1024)} %copy-done.47) | copy-start | bytes 27652
  (28 other events, 53.0 us)
where the time goes:
time: 588 us; the launch traced here: 577 us
  local copies, waits for them, and re-layouts  225 us (38%)
  blocking collectives  136 us (23%)
  matrix products  72.4 us (12%)
  between operations  72.1 us (12%)
  waiting for transfers between devices  36.9 us (6%)
  starting transfers between devices  24.2 us (4%)
  other arithmetic  10.1 us (2%)
    gather x6, local copies, waits for them, and re-layouts, local_part(): return jnp.stack([flat_grid[:, slot_re], flat_grid[:, slot_im]])  73.9 us
    psum x3, blocking collectives, projected_part(): proj_re, proj_im = lax.psum((proj_re, proj_im), 'ga')  62.5 us
    scatter x6, local copies, waits for them, and re-layouts, local_part(): flat_grid.at[:, slot_re].set(vectors[0]).at[:, slot_im].set(vectors[1])  56.4 us
    all_to_all x3, waiting for transfers between devices, real_space(): lax.all_to_all(grid_vals, 'ga', split_axis=1, concat_axis=2, tiled=True)  36.9 us
    psum x3, blocking collectives, gram_sums(): summed = lax.psum(jnp.stack(stacked), 'ga') / total_pw  35.4 us
    dot_general x12, matrix products, mix_dim(): direct = jnp.einsum(pattern, cos_table, grid_vals, precision=top_precision)  26.6 us
    dot_general x12, matrix products, mix_dim(): jnp.einsum(pattern, sin_table, quarter_turn(grid_vals), precision=top_pre...  23 us
    another operation x3, local copies, waits for them, and re-layouts, gram_sums(): summed = lax.psum(jnp.stack(stacked), 'ga') / total_pw  19.8 us
  transfers between devices with their start and end apart: 6, of which 3 were waited for; matrix products, arithmetic and copies ran while one was open for 3% of the time, Pallas kernels for 0%

commit v1 on v0

v1 whole, which is shorter than its diff:
```python
import jax
import jax.numpy as jnp
import numpy as np
from jax import lax
from jax.experimental import pallas as pl
from jax.experimental.pallas import tpu as pltpu
from jax.sharding import PartitionSpec as P

kin_unit = 0.02
small_eps = 1e-06
F32 = jnp.float32
BF16 = jnp.bfloat16
HI = lax.Precision.HIGHEST
NN = (((1,), (0,)), ((), ()))
NT = (((1,), (1,)), ((), ()))


def round_up(value, unit):
    return -(-value // unit) * unit


def split_np(table):
    hi = table.astype(np.float32).astype(jnp.bfloat16)
    lo = (table - hi.astype(np.float64)).astype(np.float32).astype(jnp.bfloat16)
    return np.stack([hi, lo])


def split(vals):
    hi = vals.astype(BF16)
    return hi, (vals - hi.astype(F32)).astype(BF16)


def mm(left, right, dims=NN):
    return lax.dot_general(left, right, dims, preferred_element_type=F32)


def mm3(left, right):
    return mm(left[0], right[0]) + (mm(left[0], right[1]) + mm(left[1], right[0]))


def call(kernel, out_shapes, scratch=()):
    return pl.pallas_call(
        kernel,
        out_shape=[jax.ShapeDtypeStruct(s, d) for s, d in out_shapes],
        scratch_shapes=list(scratch),
        compiler_params=pltpu.CompilerParams(vmem_limit_bytes=56 * 1024 * 1024),
    )


def lane_sum(vals):
    return jnp.sum(jnp.sum(vals, axis=1, keepdims=True), axis=0, keepdims=True)


def gram_form(gram, left_map, right_map, kin):
    running = 0.0
    for i, a in left_map.items():
        for j, b in right_map.items():
            running = running + a * b * gram[kin, min(i, j), max(i, j)]
    return running


def combine(terms):
    merged = {}
    for scalar, coefs in terms:
        for i, a in coefs.items():
            merged[i] = merged.get(i, 0.0) + scalar * a
    return merged


def ratio(gram, a, b, c, d, kin=False):
    return gram_form(gram, a, b, kin) / (gram_form(gram, c, d, False) + small_eps)


def pairs_of(first, last):
    return [
        (kin, i, j) for kin in (False, True) for j in range(first, last) for i in range(j + 1)
    ]


def stage_zero(gram):
    psi, ham = {0: 1.0}, {1: 1.0}
    eps = ratio(gram, psi, ham, psi, psi)
    res = combine([(1.0, ham), (-eps, psi)])
    level = ratio(gram, res, res, res, res, True)
    return eps, res, level


def stage_mid(gram):
    eps, res, _ = stage_zero(gram)
    psi, ham = {0: 1.0}, {1: 1.0}
    q = {3: 1.0, 2: -eps}
    lam = -ratio(gram, res, q, q, q)
    psi1 = combine([(1.0, psi), (lam, {2: 1.0})])
    ham1 = combine([(1.0, ham), (lam, {3: 1.0})])
    eps1 = ratio(gram, psi1, ham1, psi1, psi1)
    res1 = combine([(1.0, ham1), (-eps1, psi1)])
    change = combine([(1.0, res), (-1.0, res1)])
    weight = ratio(gram, res, change, change, change)
    step = weight * lam
    psim = combine([(1.0, psi), (step, {2: 1.0})])
    hamm = combine([(1.0, ham), (step, {3: 1.0})])
    resm = combine([(1.0, res), (-weight, change)])
    epsm = ratio(gram, psim, hamm, psim, psim)
    level = ratio(gram, resm, resm, resm, resm, True)
    return epsm, psim, hamm, resm, level


def spread(coefs, basis):
    running = 0.0
    for i, a in coefs.items():
        if not isinstance(a, float):
            a = a[0:1, 0:1]
        running = running + a * basis[i]
    return running


def precondition(residual, kinetic, level):
    x = kinetic / (1.5 * level[0:1, 0:1] + 1.0)
    numer = 27.0 + x * (18.0 + x * (12.0 + 8.0 * x))
    square = x * x
    return residual * (numer / (numer + 16.0 * square * square))


def body(coeffs, cell_map, potential, projectors, strengths, proj_atom, proj_chan):
    ga = lax.axis_size("ga")
    nband = lax.axis_size("band")
    n = potential.shape[0]
    planes = n // ga
    npw = coeffs.shape[2]
    total = npw * ga
    nproj = projectors.shape[1]
    rp = round_up(2 * planes, 8)
    lp = round_up(planes * n, 128)
    nq = lp // 128
    zp = round_up(n, 128)
    rows = ga * rp
    psl = round_up(2 * nproj, 128)
    assert psl == 128

    k = np.arange(n)
    ang = 2.0 * np.pi / n * (np.outer(k, k) % n)
    cos, sin = np.cos(ang), np.sin(ang)
    ytab = np.zeros((2 * rows, n))
    for s in range(ga):
        for yl in range(planes):
            y = s * planes + yl
            r = s * rp + yl
            ytab[r], ytab[r + planes] = cos[y], sin[y]
            ytab[rows + r], ytab[rows + r + planes] = -sin[y], cos[y]
    xf = np.block([[cos, -sin], [sin, cos]])
    xb = np.block([[cos, sin], [-sin, cos]]) / n
    zf = np.zeros((2 * zp, 2 * zp))
    zb = np.zeros((2 * zp, 2 * zp))
    zf[:n, :n], zf[:n, zp:zp + n], zf[zp:zp + n, :n], zf[zp:zp + n, zp:zp + n] = cos, sin, -sin, cos
    zb[:n, :n], zb[:n, zp:zp + n], zb[zp:zp + n, :n], zb[zp:zp + n, zp:zp + n] = cos, -sin, sin, cos
    zb = zb / n
    ytab, xf, xb, zf, zb = [jnp.asarray(split_np(t)) for t in (ytab, xf, xb, zf, zb)]

    device = lax.axis_index("ga")
    plane_num = cell_map // (n * n)
    y_index = cell_map // n % n
    z_index = cell_map % n

    def freq(idx):
        return jnp.where(2 * idx < n, idx, idx - n)

    fx, fy, fz = freq(device + ga * plane_num), freq(y_index), freq(z_index)
    kinetic = (kin_unit * (fx * fx + fy * fy + fz * fz).astype(F32))[None, :]
    ycell = y_index[None, :]
    col = (plane_num * n + z_index)[None, :]
    proj = projectors.reshape(2 * nproj, npw)
    pot = jnp.pad(jnp.transpose(potential, (1, 0, 2)), ((0, 0), (0, 0), (0, zp - n)))
    pot = pot.reshape(planes * n, zp)

    natom, nch = strengths.shape[:2]
    sym = 0.5 * (strengths + jnp.swapaxes(strengths, 1, 2))
    ahot = (proj_atom[:, None] == jnp.arange(natom)[None, :]).astype(F32)
    chot = (proj_chan[:, None] == jnp.arange(nch)[None, :]).astype(F32)
    slot = (ahot[:, :, None] * chot[:, None, :]).reshape(nproj, natom * nch)
    big = (jnp.eye(natom, dtype=F32)[:, None, :, None] * sym[:, :, None, :]).reshape(
        natom * nch, natom * nch
    )
    coup = jnp.dot(jnp.dot(slot, big, precision=HI), slot.T, precision=HI) / total
    none = jnp.zeros_like(coup)
    mix = jnp.concatenate(
        [jnp.block([[coup, none], [none, coup]]), jnp.block([[none, coup], [-coup, none]])], axis=1
    )

    def one_hot(col_ref):
        lanes = lax.broadcasted_iota(jnp.int32, (lp, npw), 0)
        return jnp.where(lanes == col_ref[...], 1.0, 0.0).astype(BF16)

    def scatter_to(out_ref, vec, tab, col_ref, proj_ref):
        wave = vec[0:1] * tab[0:rows] + vec[1:2] * tab[rows:2 * rows]
        both = jnp.concatenate(split(wave), axis=0)
        grid = mm(both, one_hot(col_ref), NT)
        grid = (grid[:rows] + grid[rows:]).reshape(ga, rp, lp)
        for q in range(nq):
            out_ref[:, q * rp:(q + 1) * rp, :] = grid[:, :, 128 * q:128 * (q + 1)]
        eight = jnp.concatenate([vec, jnp.zeros((6, npw), F32)], axis=0)
        sums = lax.dot_general(eight, proj_ref[...], NT, precision=HI, preferred_element_type=F32)
        out_ref[:, nq * rp:nq * rp + 8, :] = jnp.broadcast_to(sums[None], (ga, 8, 128))

    send_shape = ((ga, nq * rp + 8, 128), F32)

    def first_kernel(vec_ref, y_ref, col_ref, proj_ref, ytab_ref, send_ref, tab_ref):
        kk = lax.broadcasted_iota(jnp.int32, (n, npw), 0)
        hot = jnp.where(kk == y_ref[...], 1.0, 0.0).astype(BF16)
        tab_ref[...] = mm(ytab_ref[0], hot) + mm(ytab_ref[1], hot)
        scatter_to(send_ref, vec_ref[...], tab_ref[...], col_ref, proj_ref)

    def mid_kernel(in_ref, pot_ref, xf_ref, xb_ref, zf_ref, zb_ref, out_ref, sum_ref, buf_ref):
        sum_ref[...] = jnp.sum(in_ref[:, nq * rp:nq * rp + 8, :], axis=0)
        grid = jnp.concatenate([in_ref[:, q * rp:(q + 1) * rp, :] for q in range(nq)], axis=-1)
        grid = grid.reshape(rows, lp)
        for i in range(planes):
            piece = grid[:, i * n:(i + 1) * n]
            if zp > n:
                piece = jnp.concatenate([piece, jnp.zeros((rows, zp - n), F32)], axis=1)
            buf_ref[i * rows:(i + 1) * rows, :] = piece
        half = []
        for c in range(2):
            half.append(
                jnp.concatenate(
                    [buf_ref[pl.ds(c * planes + j, n, stride=rp), :] for j in range(planes)], axis=1
                )
            )
        vals = jnp.concatenate(half, axis=0)
        vals = mm3((xf_ref[0], xf_ref[1]), split(vals))

        def to_rows(v):
            re = jnp.concatenate([v[:n, j * zp:(j + 1) * zp] for j in range(planes)], axis=0)
            im = jnp.concatenate([v[n:, j * zp:(j + 1) * zp] for j in range(planes)], axis=0)
            return jnp.concatenate([re, im], axis=1)

        def to_lanes(v):
            re = jnp.concatenate([v[j * n:(j + 1) * n, :zp] for j in range(planes)], axis=1)
            im = jnp.concatenate([v[j * n:(j + 1) * n, zp:] for j in range(planes)], axis=1)
            return jnp.concatenate([re, im], axis=0)

        vals = mm3(split(to_rows(vals)), (zf_ref[0], zf_ref[1]))
        weight = pot_ref[...]
        vals = vals * jnp.concatenate([weight, weight], axis=1)
        vals = mm3(split(vals), (zb_ref[0], zb_ref[1]))
        vals = mm3((xb_ref[0], xb_ref[1]), split(to_lanes(vals)))
        if rp > 2 * planes:
            buf_ref[...] = jnp.zeros(buf_ref.shape, F32)
        for c in range(2):
            for j in range(planes):
                buf_ref[pl.ds(c * planes + j, n, stride=rp), :] = vals[
                    c * n:(c + 1) * n, j * zp:(j + 1) * zp
                ]
        pieces = [buf_ref[i * rows:(i + 1) * rows, :][:, :n] for i in range(planes)]
        if lp > planes * n:
            pieces.append(jnp.zeros((rows, lp - planes * n), F32))
        grid = jnp.concatenate(pieces, axis=1).reshape(ga, rp, lp)
        for q in range(nq):
            out_ref[:, q * rp:(q + 1) * rp, :] = grid[:, :, 128 * q:128 * (q + 1)]

    mid_call = call(
        mid_kernel,
        [((ga, nq * rp, 128), F32), ((8, 128), F32)],
        [pltpu.VMEM((n * rp, zp), F32)],
    )

    def gather_from(back_ref, sum_ref, vec, tab_ref, col_ref, proj_ref, mix_ref, kin_ref):
        grid = jnp.concatenate([back_ref[:, q * rp:(q + 1) * rp, :] for q in range(nq)], axis=-1)
        both = jnp.concatenate(split(grid.reshape(rows, lp)), axis=0)
        got = mm(both, one_hot(col_ref))
        got = (got[:rows] + got[rows:]) * (1.0 / n)
        local_re = jnp.sum(got * tab_ref[0:rows], axis=0, keepdims=True)
        local_im = jnp.sum(got * tab_ref[rows:2 * rows], axis=0, keepdims=True)
        mixed = lax.dot_general(
            sum_ref[...], mix_ref[...], NN, precision=HI, preferred_element_type=F32
        )
        straight, turned = mixed[:, :128], mixed[:, 128:]
        coef = jnp.concatenate(
            [
                straight[0:1] - turned[1:2],
                straight[1:2] + turned[0:1],
                jnp.zeros((6, 128), F32),
            ],
            axis=0,
        )
        non = lax.dot_general(coef, proj_ref[...], NN, precision=HI, preferred_element_type=F32)
        return kin_ref[...] * vec + jnp.concatenate([local_re, local_im], axis=0) + non[0:2]

    def gram_rows(basis, pairs, kin):
        sums = []
        for use_kin, i, j in pairs:
            prod = basis[i] * basis[j]
            sums.append(lane_sum(prod * kin if use_kin else prod))
        sums += [jnp.zeros((1, 1), F32)] * (round_up(len(sums), 8) - len(sums))
        return jnp.broadcast_to(jnp.concatenate(sums, axis=0), (len(sums), 128))

    def read_gram(refs):
        gram = {}
        for ref, pairs in refs:
            for at, key in enumerate(pairs):
                gram[key] = ref[at:at + 1, :] * (1.0 / total)
        return gram

    pairs_a, pairs_b = pairs_of(0, 2), pairs_of(2, 4)
    rows_a, rows_b = round_up(len(pairs_a), 8), round_up(len(pairs_b), 8)
    vec_shape = ((2, npw), F32)

    def exchange(vals):
        return lax.all_to_all(vals, "ga", split_axis=0, concat_axis=0, tiled=True)

    def local_trip(send):
        out, sums = mid_call(exchange(send), pot, xf, xb, zf, zb)
        return exchange(out), sums

    vec = coeffs.reshape(2, npw)
    send, tab = call(first_kernel, [send_shape, ((2 * rows, npw), F32)])(
        vec, ycell, col, proj, ytab
    )
    back, sums = local_trip(send)

    def third_a(back_ref, sum_ref, c_ref, tab_ref, col_ref, proj_ref, mix_ref, kin_ref, h_ref, g_ref):
        c = c_ref[...]
        h = gather_from(back_ref, sum_ref, c, tab_ref, col_ref, proj_ref, mix_ref, kin_ref)
        h_ref[...] = h
        g_ref[...] = gram_rows([c, h], pairs_a, kin_ref[...])

    h0, gram_a = call(third_a, [vec_shape, ((rows_a, 128), F32)])(
        back, sums, vec, tab, col, proj, mix, kinetic
    )
    gram_a = lax.psum(gram_a, "ga")

    def first_b(ga_ref, c_ref, h_ref, tab_ref, col_ref, proj_ref, kin_ref, send_ref, p_ref):
        gram = read_gram([(ga_ref, pairs_a)])
        _, res, level = stage_zero(gram)
        p = precondition(spread(res, [c_ref[...], h_ref[...]]), kin_ref[...], level)
        p_ref[...] = p
        scatter_to(send_ref, p, tab_ref[...], col_ref, proj_ref)

    send, p0 = call(first_b, [send_shape, vec_shape])(gram_a, vec, h0, tab, col, proj, kinetic)
    back, sums = local_trip(send)

    def third_b(
        back_ref, sum_ref, c_ref, h_ref, p_ref, tab_ref, col_ref, proj_ref, mix_ref, kin_ref, g_out, gr_ref
    ):
        p = p_ref[...]
        g = gather_from(back_ref, sum_ref, p, tab_ref, col_ref, proj_ref, mix_ref, kin_ref)
        g_out[...] = g
        gr_ref[...] = gram_rows([c_ref[...], h_ref[...], p, g], pairs_b, kin_ref[...])

    g0, gram_b = call(third_b, [vec_shape, ((rows_b, 128), F32)])(
        back, sums, vec, h0, p0, tab, col, proj, mix, kinetic
    )
    gram_b = lax.psum(gram_b, "ga")

    def first_c(
        ga_ref, gb_ref, c_ref, h_ref, p_ref, g_ref, tab_ref, col_ref, proj_ref, kin_ref,
        send_ref, all_ref, eps_ref,
    ):
        gram = read_gram([(ga_ref, pairs_a), (gb_ref, pairs_b)])
        epsm, psim, hamm, resm, level = stage_mid(gram)
        basis = [c_ref[...], h_ref[...], p_ref[...], g_ref[...]]
        p = precondition(spread(resm, basis), kin_ref[...], level)
        all_ref[0:2] = spread(psim, basis)
        all_ref[2:4] = spread(hamm, basis)
        all_ref[4:6] = p
        all_ref[6:8] = spread(resm, basis)
        eps_ref[...] = jnp.broadcast_to(epsm, (8, 128))
        scatter_to(send_ref, p, tab_ref[...], col_ref, proj_ref)

    send, trio, eps_mid = call(first_c, [send_shape, ((8, npw), F32), ((8, 128), F32)])(
        gram_a, gram_b, vec, h0, p0, g0, tab, col, proj, kinetic
    )
    others = lax.all_gather(trio, "band", axis=0, tiled=True)
    back, sums = local_trip(send)

    def third_c(
        back_ref, sum_ref, trio_ref, others_ref, tab_ref, col_ref, proj_ref, mix_ref, kin_ref, out_ref
    ):
        p = trio_ref[4:6]
        g = gather_from(back_ref, sum_ref, p, tab_ref, col_ref, proj_ref, mix_ref, kin_ref)
        own = jnp.concatenate([trio_ref[0:6], g], axis=0)
        cross = lax.dot_general(own, others_ref[...], NT, precision=HI, preferred_element_type=F32)
        mine = lax.dot_general(own, own, NT, precision=HI, preferred_element_type=F32)
        out_ref[...] = jnp.concatenate([cross, mine], axis=1)

    width = 8 * nband + 8
    (prods,) = call(third_c, [((8, width), F32)])(
        back, sums, trio, others, tab, col, proj, mix, kinetic
    )
    band = lax.axis_index("band")
    slots = jnp.where(
        jnp.arange(nband)[:, None, None] == band, jnp.concatenate([prods, eps_mid[:, :1] / ga * total], axis=1)[None], 0.0
    )
    slots = lax.psum(slots, ("band", "ga")) / total

    mine = slots[:, :, 8 * nband:8 * nband + 8]
    dots = mine.reshape(nband, 4, 2, 4, 2)
    dots = dots[:, :, 0, :, 0] + dots[:, :, 1, :, 1]
    eps_all = slots[:, 0, width]
    gram = {(False, i, j): dots[:, i, j] for i in range(4) for j in range(i, 4)}
    psim, hamm, pvec, gvec = {0: 1.0}, {1: 1.0}, {2: 1.0}, {3: 1.0}
    paired = slots[:, :, :8 * nband].reshape(nband, 4, 2, nband, 4, 2)
    paired = paired[:, :, 0, :, 3, 0] + paired[:, :, 1, :, 3, 1]
    same = jnp.arange(nband)[:, None, None] == jnp.arange(nband)[None, None, :]
    rdots = jnp.sum(jnp.where(same, paired, 0.0), axis=2)
    q = combine([(1.0, gvec), (-eps_all, pvec)])
    lam = -(rdots[:, 3] - eps_all * rdots[:, 2]) / (gram_form(gram, q, q, False) + small_eps)
    new = combine([(1.0, psim), (lam, pvec)])
    ham = combine([(1.0, hamm), (lam, gvec)])
    norm = gram_form(gram, new, new, False) + small_eps
    energy = gram_form(gram, new, ham, False) / norm
    resid = combine([(1.0, ham), (-energy, new)])
    residual_norm = gram_form(gram, resid, resid, False) / norm

    def pick(values):
        return jnp.sum(jnp.where(jnp.arange(nband) == band, values, 0.0))

    lam_own = pick(lam)
    new_bands = trio[0:2] + lam_own * trio[4:6]
    cross = jnp.sum(
        jnp.where(jnp.arange(nband)[:, None, None] == band, slots[:, :, :8 * nband], 0.0), axis=0
    ).reshape(4, 2, nband, 4, 2)
    re = cross[:, 0, :, :, 0] + cross[:, 1, :, :, 1]
    im = cross[:, 0, :, :, 1] - cross[:, 1, :, :, 0]

    def rows_of(t):
        over = t[0, :, 0] + lam * t[0, :, 2] + lam_own * (t[2, :, 0] + lam * t[2, :, 2])
        sub = t[0, :, 1] + lam * t[1, :, 2] + lam_own * (t[2, :, 1] + lam * t[3, :, 2])
        return over, sub

    over_re, sub_re = rows_of(re)
    over_im, sub_im = rows_of(im)
    correlation = jnp.stack([over_re, over_im])[:, None, :]
    subspace = jnp.stack([sub_re, sub_im])[:, None, :]
    return (
        new_bands[:, None, :],
        pick(energy)[None],
        pick(residual_norm)[None],
        correlation,
        subspace,
    )


def solution(mesh):
    placed = (
        P(None, "band", "ga"),
        P("ga"),
        P(None, "ga", None),
        P(None, None, "ga"),
        P(),
        P(),
        P(),
    )
    return jax.shard_map(
        body,
        mesh=mesh,
        in_specs=placed,
        out_specs=(
            P(None, "band", "ga"),
            P("band"),
            P("band"),
            P(None, "band", None),
            P(None, "band", None),
        ),
        check_vma=False,
    )
```

time: 588 us -> 253 us (0.43); the launches traced: 577 us -> 252 us
  local copies, waits for them, and re-layouts: 225 us -> 10.2 us
  matrix products: 72.4 us -> 0.4 us
  between operations: 72.1 us -> 0.88 us
  Pallas kernels: 0 us -> 59.6 us
  waiting for transfers between devices: 36.9 us -> 23 us
  starting transfers between devices: 24.2 us -> 12.3 us
    gather x6 -> x0, local copies, waits for them, and re-layouts: 73.9 us -> none  [local_part(): return jnp.stack([flat_grid[:, slot_re], flat_grid[:, slot_im]])]
    dot_general x71 -> x2, matrix products: 72.4 us -> 0.4 us  [the longest x1 0.24 us: body(): jnp.dot(slot, big, precision=HI)]
    pallas_call x0 -> x9, Pallas kernels: none -> 59.6 us  [the longest x3 17.9 us: local_trip(): out, sums = mid_call(exchange(send), pot, xf, xb, zf, zb)]
    scatter x6 -> x0, local copies, waits for them, and re-layouts: 56.4 us -> none  [local_part(): flat_grid.at[:, slot_re].set(vectors[0]).at[:, slot_im].set(vectors[1])]
    all_to_all x0 -> x3, blocking collectives: none -> 54.2 us  [exchange(): return lax.all_to_all(vals, 'ga', split_axis=0, concat_axis=0, tiled=True)]
    psum x7 -> x3, blocking collectives: 110 us -> 69.1 us  [the longest x1 43.6 us: body(): slots = lax.psum(slots, ('band', 'ga')) / total]
    another operation x27 -> x0, local copies, waits for them, and re-layouts: 32.5 us -> none  [the longest x3 19.8 us: gram_sums(): summed = lax.psum(jnp.stack(stacked), 'ga') / total_pw]
    all_to_all x15 -> x0, local copies, waits for them, and re-layouts: 18.5 us -> none  [the longest x9 11.1 us: local_part(): lax.all_to_all(grid_vals, 'ga', split_axis=2, concat_axis=1, tiled=True)]
  transfers between devices with their start and end apart: 6 -> 3, of which waited for: 3 -> 2; matrix products, arithmetic and copies ran while one was open for 3% -> 2% of each run, Pallas kernels for 0% -> 0%
where the time goes in v1:
time: 253 us; the launch traced here: 252 us
  blocking collectives  138 us (55%)
  Pallas kernels  59.6 us (24%)
  waiting for transfers between devices  23 us (9%)
  starting transfers between devices  12.3 us (5%)
  local copies, waits for them, and re-layouts  10.2 us (4%)
  other arithmetic  7.42 us (3%)
    all_to_all x3, blocking collectives, exchange(): return lax.all_to_all(vals, 'ga', split_axis=0, concat_axis=0, tiled=True)  54.2 us
    psum x1, blocking collectives, body(): slots = lax.psum(slots, ('band', 'ga')) / total  43.6 us
    all_to_all x3, waiting for transfers between devices, exchange(): return lax.all_to_all(vals, 'ga', split_axis=0, concat_axis=0, tiled=True)  23 us
    pallas_call x3, Pallas kernels, local_trip(): out, sums = mid_call(exchange(send), pot, xf, xb, zf, zb)  17.9 us
    all_gather x1, blocking collectives, body(): others = lax.all_gather(trio, 'band', axis=0, tiled=True)  15.1 us
    psum x1, blocking collectives, body(): gram_b = lax.psum(gram_b, 'ga')  12.8 us
    psum x1, blocking collectives, body(): gram_a = lax.psum(gram_a, 'ga')  12.7 us
    all_to_all x3, starting transfers between devices, exchange(): return lax.all_to_all(vals, 'ga', split_axis=0, concat_axis=0, tiled=True)  12.3 us
  transfers between devices with their start and end apart: 3, of which 2 were waited for; matrix products, arithmetic and copies ran while one was open for 2% of the time, Pallas kernels for 0%

profile of v1, /device:TPU:0, one launch (start us, length us, event | category | flops | bytes accessed | tf_op | source)
XLA Modules:
  0.0 252.1 jit_solution(9475044934636029834)
XLA Ops:
  0.7 1.4 copy.63
  2.1 0.7 multiply_add_fusion
  2.8 0.6 broadcast_in_dim.88.y_ref
  3.4 0.6 broadcast_in_dim.89.col_ref
  4.0 7.2 %shard_map.155 = (f32[8,224,128]{2,1,0:T(8,128)}, f32[384,2304]{1,0:T(8,128)}) custom-call(f32[2,2304]{1,0:T(2,128)} %bitcast.183, s32[1,2304]{1,0:T(1,128)} %broadcast_in_dim.88.y_ref, s32[1,2304]{1,0:T(1,128)} %broadcast_in_dim.89.col_ref, f32[128,2304]{1,0:T(8,128)} %bitcast.174, bf16[2,384,96]{2,1,0:T(8,128)(2,1)} %constant.77.clone.ytab_ref), custom_call_target="tpu_custom_call" | custom-call | tf_op jit(solution)/shard_map/pallas_call | solution.py:315
  11.2 5.2 %all-to-all-start = ((f32[8,224,128]{2,1,0:T(8,128)}), f32[8,224,128]{2,1,0:T(8,128)S(1)}, u32[]{:S(2)}, u32[]{:S(2)}) async-start(f32[8,224,128]{2,1,0:T(8,128)} %get-tuple-element.22), calls=%async_computation | async-start | bytes 1835008 | tf_op jit(solution)/shard_map/all_to_all | solution.py:308
  16.4 0.8 copy.49
  17.3 0.8 fusion.5
  18.3 0.9 pad.7
  19.2 11.2 %all-to-all-done.in_ref = f32[8,224,128]{2,1,0:T(8,128)S(1)} async-done(((f32[8,224,128]{2,1,0:T(8,128)}), f32[8,224,128]{2,1,0:T(8,128)S(1)}, u32[]{:S(2)}, u32[]{:S(2)}) %all-to-all-start) | async-done | bytes 917536 | tf_op jit(solution)/shard_map/all_to_all | solution.py:308
  30.4 0.9 copy-done
  31.3 6.0 %shard_map.156 = (f32[8,216,128]{2,1,0:T(8,128)}, f32[8,128]{1,0:T(8,128)}) custom-call(f32[8,224,128]{2,1,0:T(8,128)} %copy-done, f32[1152,128]{1,0:T(8,128)} %bitcast.180, bf16[2,192,192]{2,1,0:T(8,128)(2,1)} %constant.78.clone.xf_ref, bf16[2,192,192]{2,1,0:T(8,128)(2,1)} %constant.79.clone.xb_ref, bf16[2,256,256]{2,1,0:T(8,128)(2,1)} %constant.80.clone.zf_ref, ...), custom_call_target="tpu_custom_call" | custom-call | tf_op jit(solution)/shard_map/pallas_call | solution.py:311
  37.3 3.6 %all-to-all-start.1 = ((f32[8,216,128]{2,1,0:T(8,128)}), f32[8,216,128]{2,1,0:T(8,128)S(1)}, u32[]{:S(2)}, u32[]{:S(2)}) async-start(f32[8,216,128]{2,1,0:T(8,128)} %get-tuple-element.23), calls=%async_computation.1 | async-start | bytes 1769472 | tf_op jit(solution)/shard_map/all_to_all | solution.py:308
  40.9 0.2 fusion.7
  41.1 0.2 fusion.60
  41.4 0.6 broadcast_in_dim.90.kin_ref
  42.0 0.7 fusion.mix_ref
  42.7 11.7 %all-to-all-done.1.back_ref = f32[8,216,128]{2,1,0:T(8,128)S(1)} async-done(((f32[8,216,128]{2,1,0:T(8,128)}), f32[8,216,128]{2,1,0:T(8,128)S(1)}, u32[]{:S(2)}, u32[]{:S(2)}) %all-to-all-start.1) | async-done | bytes 884768 | tf_op jit(solution)/shard_map/all_to_all | solution.py:308
  54.4 0.9 copy-done.1
  55.3 6.5 %shard_map.157 = (f32[2,2304]{1,0:T(2,128)}, f32[8,128]{1,0:T(8,128)}) custom-call(f32[8,216,128]{2,1,0:T(8,128)} %copy-done.1, f32[8,128]{1,0:T(8,128)} %get-tuple-element.24.sum_ref, f32[2,2304]{1,0:T(2,128)} %bitcast.184, f32[384,2304]{1,0:T(8,128)} %get-tuple-element.25.tab_ref, s32[1,2304]{1,0:T(1,128)} %broadcast_in_dim.89.col_ref, ...), custom_call_target="tpu_custom_call" | custom-call | tf_op jit(solution)/shard_map/pallas_call | solution.py:326
  61.9 12.7 %psum.21.ga_ref = f32[8,128]{1,0:T(8,128)} all-reduce(f32[8,128]{1,0:T(8,128)} %get-tuple-element.26), channel_id=1, replica_groups=mesh['band'=4,'ga'=8] {'ga'}, use_global_device_ids=true, to_apply=%region_0.1 | all-reduce | flops 1024 | bytes 8192 | tf_op jit(solution)/shard_map/psum | solution.py:329
  74.5 6.8 %shard_map.158 = (f32[8,224,128]{2,1,0:T(8,128)}, f32[2,2304]{1,0:T(2,128)}) custom-call(f32[8,128]{1,0:T(8,128)} %psum.21.ga_ref, f32[2,2304]{1,0:T(2,128)} %bitcast.185, f32[2,2304]{1,0:T(2,128)} %get-tuple-element.27.h_ref, f32[384,2304]{1,0:T(8,128)} %get-tuple-element.25.tab_ref, s32[1,2304]{1,0:T(1,128)} %broadcast_in_dim.89.col_ref, ...), custom_call_target="tpu_custom_call" | custom-call | tf_op jit(solution)/shard_map/pallas_call | solution.py:338
  81.4 18.1 %all_to_all.30.in_ref = f32[8,224,128]{2,1,0:T(8,128)} all-to-all(f32[8,224,128]{2,1,0:T(8,128)} %get-tuple-element.28), channel_id=1, replica_groups=mesh['band'=4,'ga'=8] {'ga'}, dimensions={0} | all-to-all | bytes 1835008 | tf_op jit(solution)/shard_map/all_to_all | solution.py:308
  99.5 6.0 %shard_map.159 = (f32[8,216,128]{2,1,0:T(8,128)}, f32[8,128]{1,0:T(8,128)}) custom-call(f32[8,224,128]{2,1,0:T(8,128)} %all_to_all.30.in_ref, f32[1152,128]{1,0:T(8,128)} %bitcast.181, bf16[2,192,192]{2,1,0:T(8,128)(2,1)} %constant.78.clone.xf_ref, bf16[2,192,192]{2,1,0:T(8,128)(2,1)} %constant.79.clone.xb_ref, bf16[2,256,256]{2,1,0:T(8,128)(2,1)} %constant.80.clone.zf_ref, ...), custom_call_target="tpu_custom_call" | custom-call | tf_op jit(solution)/shard_map/pallas_call | solution.py:311
  105.5 17.8 %all_to_all.31.back_ref = f32[8,216,128]{2,1,0:T(8,128)} all-to-all(f32[8,216,128]{2,1,0:T(8,128)} %get-tuple-element.29), channel_id=1, replica_groups=mesh['band'=4,'ga'=8] {'ga'}, dimensions={0} | all-to-all | bytes 1769472 | tf_op jit(solution)/shard_map/all_to_all | solution.py:308
  123.3 6.6 %shard_map.160 = (f32[2,2304]{1,0:T(2,128)}, f32[16,128]{1,0:T(8,128)}) custom-call(f32[8,216,128]{2,1,0:T(8,128)} %all_to_all.31.back_ref, f32[8,128]{1,0:T(8,128)} %get-tuple-element.30.sum_ref, f32[2,2304]{1,0:T(2,128)} %bitcast.186, f32[2,2304]{1,0:T(2,128)} %get-tuple-element.27.h_ref, f32[2,2304]{1,0:T(2,128)} %get-tuple-element.31.p_ref, ...), custom_call_target="tpu_custom_call" | custom-call | tf_op jit(solution)/shard_map/pallas_call | solution.py:349
  129.8 12.8 %psum.22.gb_ref = f32[16,128]{1,0:T(8,128)} all-reduce(f32[16,128]{1,0:T(8,128)} %get-tuple-element.32), channel_id=1, replica_groups=mesh['band'=4,'ga'=8] {'ga'}, use_global_device_ids=true, to_apply=%region_1.2 | all-reduce | flops 2048 | bytes 16384 | tf_op jit(solution)/shard_map/psum | solution.py:352
  142.7 7.0 %shard_map.161 = (f32[8,224,128]{2,1,0:T(8,128)}, f32[8,2304]{1,0:T(8,128)}, f32[8,128]{1,0:T(8,128)}) custom-call(f32[8,128]{1,0:T(8,128)} %psum.21.ga_ref, f32[16,128]{1,0:T(8,128)} %psum.22.gb_ref, f32[2,2304]{1,0:T(2,128)} %bitcast.187, f32[2,2304]{1,0:T(2,128)} %get-tuple-element.27.h_ref, f32[2,2304]{1,0:T(2,128)} %get-tuple-element.31.p_ref, ...), custom_call_target="tpu_custom_call" | custom-call | tf_op jit(solution)/shard_map/pallas_call | solution.py:369
  149.7 18.3 %all_to_all.32.in_ref = f32[8,224,128]{2,1,0:T(8,128)} all-to-all(f32[8,224,128]{2,1,0:T(8,128)} %get-tuple-element.35), channel_id=1, replica_groups=mesh['band'=4,'ga'=8] {'ga'}, dimensions={0} | all-to-all | bytes 1835008 | tf_op jit(solution)/shard_map/all_to_all | solution.py:308
  168.0 6.0 %shard_map.162 = (f32[8,216,128]{2,1,0:T(8,128)}, f32[8,128]{1,0:T(8,128)}) custom-call(f32[8,224,128]{2,1,0:T(8,128)} %all_to_all.32.in_ref, f32[1152,128]{1,0:T(8,128)} %bitcast.182, bf16[2,192,192]{2,1,0:T(8,128)(2,1)} %constant.78.clone.xf_ref, bf16[2,192,192]{2,1,0:T(8,128)(2,1)} %constant.79.clone.xb_ref, bf16[2,256,256]{2,1,0:T(8,128)(2,1)} %constant.80.clone.zf_ref, ...), custom_call_target="tpu_custom_call" | custom-call | tf_op jit(solution)/shard_map/pallas_call | solution.py:311
  173.9 3.6 %all-to-all-start.5 = ((f32[8,216,128]{2,1,0:T(8,128)}), f32[8,216,128]{2,1,0:T(8,128)S(1)}, u32[]{:S(2)}, u32[]{:S(2)}) async-start(f32[8,216,128]{2,1,0:T(8,128)} %get-tuple-element.36), calls=%async_computation.5 | async-start | bytes 1769472 | tf_op jit(solution)/shard_map/all_to_all | solution.py:308
  177.5 15.1 %all_gather.3.others_ref = f32[32,2304]{1,0:T(8,128)} all-gather(f32[8,2304]{1,0:T(8,128)S(1)} %copy-done.4), channel_id=1, replica_groups=mesh['band'=4,'ga'=8] {'band'}, dimensions={0}, use_global_device_ids=true | all-gather | bytes 368640 | tf_op jit(solution)/shard_map/all_gather | solution.py:372
  192.6 0.9 copy-done.2
  193.6 7.5 %shard_map.163 = f32[8,40]{1,0:T(8,128)} custom-call(f32[8,216,128]{2,1,0:T(8,128)} %copy-done.2, f32[8,128]{1,0:T(8,128)} %get-tuple-element.37.sum_ref, f32[8,2304]{1,0:T(8,128)} %get-tuple-element.34.trio_ref, f32[32,2304]{1,0:T(8,128)} %all_gather.3.others_ref, f32[384,2304]{1,0:T(8,128)} %get-tuple-element.25.tab_ref, ...), custom_call_target="tpu_custom_call" | custom-call | tf_op jit(solution)/shard_map/pallas_call | solution.py:386
  201.0 0.8 pad_maximum_fusion
  201.9 43.6 %psum.23 = f32[4,8,41]{0,2,1:T(8,128)S(1)} all-reduce(f32[4,8,41]{0,2,1:T(8,128)S(1)} %broadcast_select_fusion), channel_id=1, replica_groups=mesh['band'=4,'ga'=8] {'band','ga'}, use_global_device_ids=true, to_apply=%region_2.3 | all-reduce | flops 1312 | bytes 10496 | tf_op jit(solution)/shard_map/psum | solution.py:393
  245.9 0.2 slice_reduce_fusion.16
  246.5 0.2 slice_reduce_fusion.26
  246.7 0.6 select_reduce_fusion.1
  247.4 0.7 add_bitcast_fusion
  248.0 0.6 copy.54
  248.8 0.2 fusion.4
  249.0 0.3 slice_reduce_fusion.7
  249.3 0.3 slice_reduce_fusion.3
  249.6 0.7 fusion.37
  250.3 0.7 fusion.33
  250.9 0.6 pad_maximum_fusion.1
  251.5 0.6 pad_maximum_fusion.2
  (41 shorter events, 1.3 us)
Async XLA Ops:
  0.6 17.6 %copy-start.3 = (f32[96,12,96]{2,0,1:T(8,128)S(1)}, f32[96,12,96]{2,0,1:T(8,128)}, u32[]{:S(2)}) copy-start(f32[96,12,96]{2,0,1:T(8,128)} %param.14) | copy-start | bytes 1327108
  0.6 18.5 %copy-start.8 = (s32[64]{0:T(128)S(1)}, s32[64]{0:T(128)}, u32[]{:S(2)}) copy-start(s32[64]{0:T(128)} %param.17) | copy-start | bytes 772
  0.7 18.5 %copy-start.9 = (s32[64]{0:T(128)S(1)}, s32[64]{0:T(128)}, u32[]{:S(2)}) copy-start(s32[64]{0:T(128)} %param.18) | copy-start | bytes 772
  11.2 19.2 %all-to-all-start = ((f32[8,224,128]{2,1,0:T(8,128)}), f32[8,224,128]{2,1,0:T(8,128)S(1)}, u32[]{:S(2)}, u32[]{:S(2)}) async-start(f32[8,224,128]{2,1,0:T(8,128)} %get-tuple-element.22), calls=%async_computation | async-start | bytes 1835008 | tf_op jit(solution)/shard_map/all_to_all | solution.py:308
  16.4 24.9 %copy-start.6 = (s32[2304]{0:T(1024)S(1)}, s32[2304]{0:T(1024)}, u32[]{:S(2)}) copy-start(s32[2304]{0:T(1024)} %param.13) | copy-start | bytes 27652
  30.4 0.9 copy-start
  37.3 17.1 %all-to-all-start.1 = ((f32[8,216,128]{2,1,0:T(8,128)}), f32[8,216,128]{2,1,0:T(8,128)S(1)}, u32[]{:S(2)}, u32[]{:S(2)}) async-start(f32[8,216,128]{2,1,0:T(8,128)} %get-tuple-element.23), calls=%async_computation.1 | async-start | bytes 1769472 | tf_op jit(solution)/shard_map/all_to_all | solution.py:308
  54.4 0.9 copy-start.1
  149.7 27.9 %copy-start.4 = (f32[8,2304]{1,0:T(8,128)S(1)}, f32[8,2304]{1,0:T(8,128)}, u32[]{:S(2)}) copy-start(f32[8,2304]{1,0:T(8,128)} %get-tuple-element.34.trio_ref) | copy-start | bytes 221188
  149.7 42.9 %copy-start.7 = (f32[8,128]{1,0:T(8,128)S(1)}, f32[8,128]{1,0:T(8,128)}, u32[]{:S(2)}) copy-start(f32[8,128]{1,0:T(8,128)} %get-tuple-element.38) | copy-start | bytes 12292
  173.9 18.7 %all-to-all-start.5 = ((f32[8,216,128]{2,1,0:T(8,128)}), f32[8,216,128]{2,1,0:T(8,128)S(1)}, u32[]{:S(2)}, u32[]{:S(2)}) async-start(f32[8,216,128]{2,1,0:T(8,128)} %get-tuple-element.36), calls=%async_computation.5 | async-start | bytes 1769472 | tf_op jit(solution)/shard_map/all_to_all | solution.py:308
  192.6 0.9 copy-start.2
  193.6 53.8 %copy-start.5 = (f32[8,2304]{1,0:T(8,128)S(1)}, f32[8,2304]{1,0:T(8,128)}, u32[]{:S(2)}) copy-start(f32[8,2304]{1,0:T(8,128)} %get-tuple-element.34.trio_ref) | copy-start | bytes 221188
